TPU v7x, 32 devices: a whole 2x2x4 slice. The times are simulated.
32 devices in a mesh: seq: 4 (over y, x), col: 8 (over z, core).
Axes of the slice: x: 2, y: 2, z: 4, core: 2. Of those that a mesh axis runs over, the one named last changes fastest.
Arguments:
- alignment: bfloat16 [32, 128, 256], P('seq', 'col')
- row_query: bfloat16 [256, 128], replicated
- row_key: bfloat16 [256, 128], replicated
- row_value: bfloat16 [256, 128], replicated, may hold values from -0.375 to 0.375
- row_output: bfloat16 [128, 256], replicated, may hold values from -0.5 to 0.5
- column_query: bfloat16 [256, 128], replicated
- column_key: bfloat16 [256, 128], replicated
- column_value: bfloat16 [256, 128], replicated, may hold values from -0.375 to 0.375
- column_output: bfloat16 [128, 256], replicated, may hold values from -0.5 to 0.5
Outputs:
- row_update: bfloat16 [32, 128, 256], P('seq', 'col')
- layer_output: bfloat16 [32, 128, 256], P('seq', 'col')
All inputs are finite; a program needn't handle non-finite values.
Results may differ from a plain program's by a relative error of at most 0.014.
Values may be sent and summed in bfloat16 or wider, within the bound.
No kernel may reach another device: no remote copies, remote signals or barrier semaphores. Data moves between devices by JAX's collectives and lax.ppermute only.
A program may use at most 64 MiB of HBM per device.

v0:
```python
import jax
import jax.numpy as jnp
from jax import lax
from jax.sharding import PartitionSpec as P

HEADS = 4
HEAD_DIM = 32


def layer_norm(field):
    values = field.astype(jnp.float32)
    mean = jnp.mean(values, axis=-1, keepdims=True)
    centred = values - mean
    variance = jnp.mean(centred * centred, axis=-1, keepdims=True)
    return (centred * lax.rsqrt(variance + 1e-05)).astype(jnp.bfloat16)


def project(field, weight):
    return jnp.dot(field, weight, preferred_element_type=jnp.float32)


def column_attend(queries, keys, values):
    seq_rows, columns, inner = queries.shape
    query_heads = queries.reshape(seq_rows, columns, HEADS, HEAD_DIM)
    key_heads = keys.reshape(keys.shape[0], columns, HEADS, HEAD_DIM)
    value_heads = values.reshape(values.shape[0], columns, HEADS, HEAD_DIM)
    scores = jnp.einsum(
        "schd,tchd->chst", query_heads, key_heads, preferred_element_type=jnp.float32
    ) * float(HEAD_DIM) ** (-0.5)
    weights = jax.nn.softmax(scores, axis=-1).astype(jnp.bfloat16)
    context = jnp.einsum(
        "chst,tchd->schd", weights, value_heads, preferred_element_type=jnp.float32
    )
    return context.reshape(seq_rows, columns, inner).astype(jnp.bfloat16)


def on_device(
    alignment,
    row_query,
    row_key,
    row_value,
    row_output,
    column_query,
    column_key,
    column_value,
    column_output,
):
    seq_dev, col_dev, width = alignment.shape
    inner = row_query.shape[1]
    scale = float(HEAD_DIM * seq_dev * lax.axis_size("seq")) ** (-0.5)
    normed = layer_norm(alignment)
    queries = project(normed, row_query).astype(jnp.bfloat16)
    keys = project(normed, row_key).astype(jnp.bfloat16)
    values = project(normed, row_value).astype(jnp.bfloat16)
    query_heads = queries.reshape(seq_dev, col_dev, HEADS, HEAD_DIM)
    piece = lax.all_gather(keys, "col", axis=1, tiled=True)
    piece_heads = piece.reshape(seq_dev, piece.shape[1], HEADS, HEAD_DIM)
    partial_value = jnp.einsum(
        "sihd,sjhd->hij", query_heads, piece_heads, preferred_element_type=jnp.float32
    )
    logits = lax.psum(partial_value, "seq") * scale
    probs = jax.nn.softmax(logits, axis=-1).astype(jnp.bfloat16)
    piece = lax.all_gather(values, "col", axis=1, tiled=True)
    piece_heads = piece.reshape(seq_dev, piece.shape[1], HEADS, HEAD_DIM)
    context = jnp.einsum("hij,sjhd->sihd", probs, piece_heads, preferred_element_type=jnp.float32)
    context = context.reshape(seq_dev, col_dev, inner).astype(jnp.bfloat16)
    row_update = project(context, row_output).astype(jnp.bfloat16)
    middle = (alignment.astype(jnp.float32) + row_update.astype(jnp.float32)).astype(jnp.bfloat16)
    column_normed = layer_norm(middle)
    column_queries = project(column_normed, column_query).astype(jnp.bfloat16)
    column_keys = project(column_normed, column_key).astype(jnp.bfloat16)
    column_values = project(column_normed, column_value).astype(jnp.bfloat16)
    every_keys, every_values = (
        lax.all_gather(column_keys, "seq", axis=0, tiled=True),
        lax.all_gather(column_values, "seq", axis=0, tiled=True),
    )
    column_context = column_attend(column_queries, every_keys, every_values)
    layer_output = (middle.astype(jnp.float32) + project(column_context, column_output)).astype(
        jnp.bfloat16
    )
    return (row_update, layer_output)


def solution(mesh):
    return jax.shard_map(
        on_device,
        mesh=mesh,
        in_specs=(P("seq", "col", None), P(), P(), P(), P(), P(), P(), P(), P()),
        out_specs=(P("seq", "col", None), P("seq", "col", None)),
        check_vma=False,
    )
```

profile of v0, /device:TPU:0, one launch (start us, length us, event | category | flops | bytes accessed | tf_op | source)
XLA Modules:
  0.0 75.1 jit_solution(4044517943388862189)
XLA Ops:
  0.7 1.0 %convert_reduce_fusion.1 = f32[8,16]{1,0:T(8,128)S(1)} fusion(bf16[8,16,256]{2,1,0:T(8,128)(2,1)} %param.9), kind=kLoop, calls=%fused_computation.30 | loop fusion | flops 65408 | bytes 66048 | tf_op jit(solution)/shard_map/reduce_sum | solution.py:12
  1.7 0.2 fusion.19
  1.9 0.2 convolution_convert_fusion.6
  2.1 15.9 %all_gather.13 = bf16[8,128,128]{2,1,0:T(8,128)(2,1)S(1)} all-gather(bf16[8,16,128]{2,1,0:T(8,128)(2,1)S(1)} %convolution_convert_fusion.6), channel_id=1, replica_groups=mesh['seq'=4,'col'=8] {'col'}, dimensions={1}, use_global_device_ids=true | all-gather | bytes 294912 | tf_op jit(solution)/shard_map/all_gather | solution.py:56
  18.0 0.2 copy.36
  18.2 0.7 copy-done.4
  18.8 0.2 convolution_convert_fusion.7
  19.2 0.2 convolution_bitcast_fusion
  19.4 16.4 %psum.7 = f32[4,16,128]{2,1,0:T(8,128)S(1)} all-reduce(f32[4,16,128]{2,1,0:T(8,128)S(1)} %convolution_bitcast_fusion), channel_id=1, replica_groups=mesh['seq'=4,'col'=8] {'seq'}, use_global_device_ids=true, to_apply=%region_2.0 | all-reduce | flops 8192 | bytes 65536 | tf_op jit(solution)/shard_map/psum | solution.py:61
  35.9 0.2 fusion.51
  36.0 0.2 convolution_convert_fusion.8
  36.3 14.3 %all_gather.12 = bf16[8,128,128]{2,1,0:T(8,128)(2,1)S(1)} all-gather(bf16[8,16,128]{2,1,0:T(8,128)(2,1)S(1)} %convolution_convert_fusion.8), channel_id=1, replica_groups=mesh['seq'=4,'col'=8] {'col'}, dimensions={1}, use_global_device_ids=true | all-gather | bytes 294912 | tf_op jit(solution)/shard_map/all_gather | solution.py:63
  50.6 0.2 copy.35
  50.8 0.5 fusion.5
  51.2 0.1 copy.40
  51.5 0.8 %convert_reduce_fusion = (f32[8,16]{1,0:T(8,128)S(1)}, bf16[8,16,256]{2,1,0:T(8,128)(2,1)S(1)}, bf16[8,16,256]{2,1,0:T(8,128)(2,1)}) fusion(bf16[8,16,256]{2,1,0:T(8,128)(2,1)S(1)} %copy-done.1, bf16[8,16,128]{2,1,0:T(8,128)(2,1)S(1)} %convert_element_type.76, bf16[128,256]{1,0:T(8,128)(2,1)S(1)} %copy-done), kind=kOutput, calls=%fused_computation.27 | convolution fusion | flops 8617856 | bytes 295424 | tf_op jit(solution)/shard_map/dot_general | solution.py:19
  52.3 0.2 fusion.17
  52.5 0.6 copy-done.6
  53.1 0.2 convolution_convert_fusion.4
  53.5 0.7 copy-done.7
  54.2 0.2 convolution_convert_fusion.3
  54.4 7.5 %all_gather.15 = bf16[32,16,128]{2,1,0:T(8,128)(2,1)S(1)} all-gather(bf16[8,16,128]{2,1,0:T(8,128)(2,1)S(1)} %convolution_convert_fusion.3), channel_id=1, replica_groups=mesh['seq'=4,'col'=8] {'seq'}, dimensions={0}, use_global_device_ids=true | all-gather | bytes 163840 | tf_op jit(solution)/shard_map/all_gather | solution.py:74
  62.0 0.2 reshape.59
  62.2 0.5 convolution_multiply_fusion
  62.7 0.3 fusion.52
  63.0 0.6 copy-done.8
  63.5 0.2 convolution_convert_fusion.5
  63.8 8.4 %all_gather.14 = bf16[32,16,128]{2,1,0:T(8,128)(2,1)S(1)} all-gather(bf16[8,16,128]{2,1,0:T(8,128)(2,1)S(1)} %convolution_convert_fusion.5), channel_id=1, replica_groups=mesh['seq'=4,'col'=8] {'seq'}, dimensions={0}, use_global_device_ids=true | all-gather | bytes 163840 | tf_op jit(solution)/shard_map/all_gather | solution.py:75
  72.1 0.2 reshape.57
  72.4 1.0 %fusion.4 = bf16[8,16,4,32]{3,0,2,1:T(8,128)(2,1)S(1)} fusion(bf16[32,16,4,32]{3,2,1,0:T(4,128)(2,1)S(1)} %reshape.57, f32[16,4,8]{2,1,0:T(4,128)S(1)} %fusion.52, f32[16,4,8,32]{3,2,1,0:T(8,128)S(1)} %convolution_multiply_fusion), kind=kOutput, calls=%fused_computation.7 | convolution fusion | flops 1114655 | bytes 231424 | tf_op jit(solution)/shard_map/chst,tchd->schd/dot_general | solution.py:31
  73.6 0.7 copy-done.2
  74.3 0.8 %fusion.6 = bf16[8,16,256]{2,1,0:T(8,128)(2,1)} fusion(bf16[8,16,128]{2,1,0:T(8,128)(2,1)S(1)} %convert_element_type.88, bf16[8,16,256]{2,1,0:T(8,128)(2,1)S(1)} %get-tuple-element.3, bf16[128,256]{1,0:T(8,128)(2,1)S(1)} %copy-done.2), kind=kOutput, calls=%fused_computation.11 | convolution fusion | flops 8486912 | bytes 229376 | tf_op jit(solution)/shard_map/dot_general | solution.py:19
  (22 shorter events, 0.6 us)
Async XLA Ops:
  0.6 50.9 %copy-start = (bf16[128,256]{1,0:T(8,128)(2,1)S(1)}, bf16[128,256]{1,0:T(8,128)(2,1)}, u32[]{:S(2)}) copy-start(bf16[128,256]{1,0:T(8,128)(2,1)} %param.13) | copy-start | bytes 196612
  0.6 1.0 %copy-start.1 = (bf16[8,16,256]{2,1,0:T(8,128)(2,1)S(1)}, bf16[8,16,256]{2,1,0:T(8,128)(2,1)}, u32[]{:S(2)}) copy-start(bf16[8,16,256]{2,1,0:T(8,128)(2,1)} %param.9) | copy-start | bytes 196612
  0.7 1.2 %copy-start.3 = (bf16[256,128]{1,0:T(8,128)(2,1)S(1)}, bf16[256,128]{1,0:T(8,128)(2,1)}, u32[]{:S(2)}) copy-start(bf16[256,128]{1,0:T(8,128)(2,1)} %param.11) | copy-start | bytes 196612
  18.0 0.8 %copy-start.4 = (bf16[256,128]{1,0:T(8,128)(2,1)S(1)}, bf16[256,128]{1,0:T(8,128)(2,1)}, u32[]{:S(2)}) copy-start(bf16[256,128]{1,0:T(8,128)(2,1)} %param.10) | copy-start | bytes 196612
  19.4 16.6 %copy-start.5 = (bf16[256,128]{1,0:T(8,128)(2,1)S(1)}, bf16[256,128]{1,0:T(8,128)(2,1)}, u32[]{:S(2)}) copy-start(bf16[256,128]{1,0:T(8,128)(2,1)} %param.12) | copy-start | bytes 196612
  52.3 0.8 %copy-start.6 = (bf16[256,128]{1,0:T(8,128)(2,1)S(1)}, bf16[256,128]{1,0:T(8,128)(2,1)}, u32[]{:S(2)}) copy-start(bf16[256,128]{1,0:T(8,128)(2,1)} %param.14) | copy-start | bytes 196612
  53.4 0.8 %copy-start.7 = (bf16[256,128]{1,0:T(8,128)(2,1)S(1)}, bf16[256,128]{1,0:T(8,128)(2,1)}, u32[]{:S(2)}) copy-start(bf16[256,128]{1,0:T(8,128)(2,1)} %param.15) | copy-start | bytes 196612
  62.7 0.8 %copy-start.8 = (bf16[256,128]{1,0:T(8,128)(2,1)S(1)}, bf16[256,128]{1,0:T(8,128)(2,1)}, u32[]{:S(2)}) copy-start(bf16[256,128]{1,0:T(8,128)(2,1)} %param.16) | copy-start | bytes 196612
  73.4 0.8 %copy-start.2 = (bf16[128,256]{1,0:T(8,128)(2,1)S(1)}, bf16[128,256]{1,0:T(8,128)(2,1)}, u32[]{:S(2)}) copy-start(bf16[128,256]{1,0:T(8,128)(2,1)} %param.17) | copy-start | bytes 196612
where the time goes:
time: 75.6 us; the launch traced here: 75.1 us
  blocking collectives  62.6 us (83%)
  matrix products  5.07 us (7%)
  local copies, waits for them, and re-layouts  4.82 us (6%)
  other arithmetic  1.75 us (2%)
  between operations  0.86 us (1%)
    psum x1, blocking collectives, on_device(): logits = lax.psum(partial_value, 'seq') * scale  16.4 us
    all_gather x1, blocking collectives, on_device(): piece = lax.all_gather(keys, 'col', axis=1, tiled=True)  15.9 us
    all_gather x1, blocking collectives, on_device(): piece = lax.all_gather(values, 'col', axis=1, tiled=True)  14.3 us
    all_gather x1, blocking collectives, on_device(): lax.all_gather(column_values, 'seq', axis=0, tiled=True)  8.37 us
    all_gather x1, blocking collectives, on_device(): lax.all_gather(column_keys, 'seq', axis=0, tiled=True)  7.55 us
    unnamed x18, local copies, waits for them, and re-layouts  3.34 us
    dot_general x8, matrix products, project(): return jnp.dot(field, weight, preferred_element_type=jnp.float32)  2.87 us

commit v1 on v0

--- a/solution.py
+++ b/solution.py
@@ -60,7 +60,12 @@
     )
     logits = lax.psum(partial_value, "seq") * scale
     probs = jax.nn.softmax(logits, axis=-1).astype(jnp.bfloat16)
-    piece = lax.all_gather(values, "col", axis=1, tiled=True)
+    ring = [values]
+    for hop in range(7):
+        ring.append(lax.ppermute(ring[-1], "col", [(dev, (dev + 1) % 8) for dev in range(8)]))
+    piece = jnp.roll(
+        jnp.concatenate(ring[::-1], axis=1), (lax.axis_index("col") + 1) * ring[0].shape[1], axis=1
+    )
     piece_heads = piece.reshape(seq_dev, piece.shape[1], HEADS, HEAD_DIM)
     context = jnp.einsum("hij,sjhd->sihd", probs, piece_heads, preferred_element_type=jnp.float32)
     context = context.reshape(seq_dev, col_dev, inner).astype(jnp.bfloat16)

time: 75.6 us -> 86.3 us (1.14)
  waiting for transfers between devices: 0 us -> 25.5 us
  blocking collectives: 62.6 us -> 47.2 us
  starting transfers between devices: 0 us -> 1.01 us
    ppermute x0 -> x7, waiting for transfers between devices: none -> 25.5 us  [on_device(): lax.ppermute(ring[-1], 'col', [(dev, (dev + 1) % 8) for dev in range(8)])]
    all_gather x1 -> x0, blocking collectives: 14.3 us -> none  [on_device(): piece = lax.all_gather(values, 'col', axis=1, tiled=True)]
    all_gather x1, blocking collectives: 15.9 us -> 14.3 us  [on_device(): piece = lax.all_gather(keys, 'col', axis=1, tiled=True)]
    ppermute x0 -> x7, starting transfers between devices: none -> 1.01 us  [on_device(): lax.ppermute(ring[-1], 'col', [(dev, (dev + 1) % 8) for dev in range(8)])]
    unnamed x18 -> x33, local copies, waits for them, and re-layouts: 3.34 us -> 2.84 us
  transfers between devices with their start and end apart: 0 -> 7, of which waited for: 0 -> 5; matrix products, arithmetic and copies ran while one was open for 0% -> 1% of each run, Pallas kernels for 0% -> 0%
where the time goes in v1:
time: 86.3 us; the launch traced here: 85.9 us
  blocking collectives  47.2 us (55%)
  waiting for transfers between devices  25.5 us (30%)
  matrix products  5.06 us (6%)
  local copies, waits for them, and re-layouts  4.36 us (5%)
  other arithmetic  1.75 us (2%)
  starting transfers between devices  1.01 us (1%)
  between operations  0.98 us (1%)
    ppermute x7, waiting for transfers between devices, on_device(): lax.ppermute(ring[-1], 'col', [(dev, (dev + 1) % 8) for dev in range(8)])  25.5 us
    psum x1, blocking collectives, on_device(): logits = lax.psum(partial_value, 'seq') * scale  16.8 us
    all_gather x1, blocking collectives, on_device(): piece = lax.all_gather(keys, 'col', axis=1, tiled=True)  14.3 us
    all_gather x1, blocking collectives, on_device(): lax.all_gather(column_values, 'seq', axis=0, tiled=True)  8.38 us
    all_gather x1, blocking collectives, on_device(): lax.all_gather(column_keys, 'seq', axis=0, tiled=True)  7.71 us
    dot_general x8, matrix products, project(): return jnp.dot(field, weight, preferred_element_type=jnp.float32)  2.86 us
    unnamed x33, local copies, waits for them, and re-layouts  2.84 us
  transfers between devices with their start and end apart: 7, of which 5 were waited for; matrix products, arithmetic and copies ran while one was open for 1% of the time, Pallas kernels for 0%

profile of v1, /device:TPU:0, one launch (start us, length us, event | category | flops | bytes accessed | tf_op | source)
XLA Modules:
  0.0 85.9 jit_solution(8940645771085927193)
XLA Ops:
  0.7 1.0 %convert_reduce_fusion.1 = f32[8,16]{1,0:T(8,128)S(1)} fusion(bf16[8,16,256]{2,1,0:T(8,128)(2,1)} %param.9), kind=kLoop, calls=%fused_computation.30 | loop fusion | flops 65408 | bytes 66048 | tf_op jit(solution)/shard_map/reduce_sum | solution.py:12
  1.9 0.2 convolution_convert_fusion.8
  2.1 0.5 collective-permute-start
  2.7 5.6 %collective-permute-done = bf16[8,16,128]{2,1,0:T(8,128)(2,1)S(1)} collective-permute-done((bf16[8,16,128]{2,1,0:T(8,128)(2,1)S(1)}, bf16[8,16,128]{2,1,0:T(8,128)(2,1)S(1)}, u32[]{:S(2)}, u32[]{:S(2)}) %collective-permute-start) | collective-permute-done | bytes 32800 | tf_op jit(solution)/shard_map/ppermute | solution.py:65
  8.3 5.1 %collective-permute-done.1 = bf16[8,16,128]{2,1,0:T(8,128)(2,1)S(1)} collective-permute-done((bf16[8,16,128]{2,1,0:T(8,128)(2,1)S(1)}, bf16[8,16,128]{2,1,0:T(8,128)(2,1)S(1)}, u32[]{:S(2)}, u32[]{:S(2)}) %collective-permute-start.1) | collective-permute-done | bytes 32800 | tf_op jit(solution)/shard_map/ppermute | solution.py:65
  13.4 0.2 convolution_convert_fusion.6
  13.7 4.9 %collective-permute-done.2 = bf16[8,16,128]{2,1,0:T(8,128)(2,1)S(1)} collective-permute-done((bf16[8,16,128]{2,1,0:T(8,128)(2,1)S(1)}, bf16[8,16,128]{2,1,0:T(8,128)(2,1)S(1)}, u32[]{:S(2)}, u32[]{:S(2)}) %collective-permute-start.2) | collective-permute-done | bytes 32800 | tf_op jit(solution)/shard_map/ppermute | solution.py:65
  18.6 0.2 convolution_convert_fusion.7
  18.8 4.9 %collective-permute-done.3 = bf16[8,16,128]{2,1,0:T(8,128)(2,1)S(1)} collective-permute-done((bf16[8,16,128]{2,1,0:T(8,128)(2,1)S(1)}, bf16[8,16,128]{2,1,0:T(8,128)(2,1)S(1)}, u32[]{:S(2)}, u32[]{:S(2)}) %collective-permute-start.3) | collective-permute-done | bytes 32800 | tf_op jit(solution)/shard_map/ppermute | solution.py:65
  23.7 14.3 %all_gather.9 = bf16[8,128,128]{2,1,0:T(8,128)(2,1)S(1)} all-gather(bf16[8,16,128]{2,1,0:T(8,128)(2,1)S(1)} %convolution_convert_fusion.6), channel_id=1, replica_groups=mesh['seq'=4,'col'=8] {'col'}, dimensions={1}, use_global_device_ids=true | all-gather | bytes 294912 | tf_op jit(solution)/shard_map/all_gather | solution.py:56
  38.3 0.4 collective-permute-start.5
  38.7 0.2 convolution_bitcast_fusion
  38.9 16.8 %psum.7 = f32[4,16,128]{2,1,0:T(8,128)S(1)} all-reduce(f32[4,16,128]{2,1,0:T(8,128)S(1)} %convolution_bitcast_fusion), channel_id=1, replica_groups=mesh['seq'=4,'col'=8] {'seq'}, use_global_device_ids=true, to_apply=%region_2.0 | all-reduce | flops 8192 | bytes 65536 | tf_op jit(solution)/shard_map/psum | solution.py:61
  56.0 5.0 %collective-permute-done.6 = bf16[8,16,128]{2,1,0:T(8,128)(2,1)S(1)} collective-permute-done((bf16[8,16,128]{2,1,0:T(8,128)(2,1)S(1)}, bf16[8,16,128]{2,1,0:T(8,128)(2,1)S(1)}, u32[]{:S(2)}, u32[]{:S(2)}) %collective-permute-start.6) | collective-permute-done | bytes 32800 | tf_op jit(solution)/shard_map/ppermute | solution.py:65
  61.2 0.2 copy.34
  61.4 0.5 fusion.5
  62.1 0.8 convert_reduce_fusion
  63.1 0.6 copy-done.6
  63.8 0.2 convolution_convert_fusion.4
  64.1 0.7 copy-done.7
  64.8 0.2 convolution_convert_fusion.3
  65.1 7.7 %all_gather.11 = bf16[32,16,128]{2,1,0:T(8,128)(2,1)S(1)} all-gather(bf16[8,16,128]{2,1,0:T(8,128)(2,1)S(1)} %convolution_convert_fusion.3), channel_id=1, replica_groups=mesh['seq'=4,'col'=8] {'seq'}, dimensions={0}, use_global_device_ids=true | all-gather | bytes 163840 | tf_op jit(solution)/shard_map/all_gather | solution.py:79
  72.8 0.2 reshape.59
  73.0 0.5 convolution_multiply_fusion
  73.5 0.3 fusion.52
  73.8 0.6 copy-done.8
  74.3 0.2 convolution_convert_fusion.5
  74.6 8.4 %all_gather.10 = bf16[32,16,128]{2,1,0:T(8,128)(2,1)S(1)} all-gather(bf16[8,16,128]{2,1,0:T(8,128)(2,1)S(1)} %convolution_convert_fusion.5), channel_id=1, replica_groups=mesh['seq'=4,'col'=8] {'seq'}, dimensions={0}, use_global_device_ids=true | all-gather | bytes 163840 | tf_op jit(solution)/shard_map/all_gather | solution.py:80
  82.9 0.2 reshape.57
  83.2 1.0 %fusion.4 = bf16[8,16,4,32]{3,0,2,1:T(8,128)(2,1)S(1)} fusion(bf16[32,16,4,32]{3,2,1,0:T(4,128)(2,1)S(1)} %reshape.57, f32[16,4,8]{2,1,0:T(4,128)S(1)} %fusion.52, f32[16,4,8,32]{3,2,1,0:T(8,128)S(1)} %convolution_multiply_fusion), kind=kOutput, calls=%fused_computation.7 | convolution fusion | flops 1114655 | bytes 231424 | tf_op jit(solution)/shard_map/chst,tchd->schd/dot_general | solution.py:31
  84.4 0.7 copy-done.2
  85.1 0.8 fusion.6
  (52 shorter events, 1.6 us)
Async XLA Ops:
  0.6 61.5 %copy-start = (bf16[128,256]{1,0:T(8,128)(2,1)S(1)}, bf16[128,256]{1,0:T(8,128)(2,1)}, u32[]{:S(2)}) copy-start(bf16[128,256]{1,0:T(8,128)(2,1)} %param.13) | copy-start | bytes 196612
  0.6 1.0 %copy-start.1 = (bf16[8,16,256]{2,1,0:T(8,128)(2,1)S(1)}, bf16[8,16,256]{2,1,0:T(8,128)(2,1)}, u32[]{:S(2)}) copy-start(bf16[8,16,256]{2,1,0:T(8,128)(2,1)} %param.9) | copy-start | bytes 196612
  0.7 1.2 %copy-start.3 = (bf16[256,128]{1,0:T(8,128)(2,1)S(1)}, bf16[256,128]{1,0:T(8,128)(2,1)}, u32[]{:S(2)}) copy-start(bf16[256,128]{1,0:T(8,128)(2,1)} %param.12) | copy-start | bytes 196612
  1.9 11.6 %copy-start.4 = (bf16[256,128]{1,0:T(8,128)(2,1)S(1)}, bf16[256,128]{1,0:T(8,128)(2,1)}, u32[]{:S(2)}) copy-start(bf16[256,128]{1,0:T(8,128)(2,1)} %param.11) | copy-start | bytes 196612
  2.1 16.5 %copy-start.5 = (bf16[256,128]{1,0:T(8,128)(2,1)S(1)}, bf16[256,128]{1,0:T(8,128)(2,1)}, u32[]{:S(2)}) copy-start(bf16[256,128]{1,0:T(8,128)(2,1)} %param.10) | copy-start | bytes 196612
  2.1 6.2 %collective-permute-start = (bf16[8,16,128]{2,1,0:T(8,128)(2,1)S(1)}, bf16[8,16,128]{2,1,0:T(8,128)(2,1)S(1)}, u32[]{:S(2)}, u32[]{:S(2)}) collective-permute-start(bf16[8,16,128]{2,1,0:T(8,128)(2,1)S(1)} %convolution_convert_fusion.8), channel_id=1, source_target_pairs={{0,1},{1,2},{2,3},{3,4},{4,5},{5,6},{6,7},{7,0},{8,9},{9,10},{10,1... | collective-permute-start | bytes 98312 | tf_op jit(solution)/shard_map/ppermute | solution.py:65
  8.3 5.1 %collective-permute-start.1 = (bf16[8,16,128]{2,1,0:T(8,128)(2,1)S(1)}, bf16[8,16,128]{2,1,0:T(8,128)(2,1)S(1)}, u32[]{:S(2)}, u32[]{:S(2)}) collective-permute-start(bf16[8,16,128]{2,1,0:T(8,128)(2,1)S(1)} %collective-permute-done), channel_id=1, source_target_pairs={{0,1},{1,2},{2,3},{3,4},{4,5},{5,6},{6,7},{7,0},{8,9},{9,10},{10,1... | collective-permute-start | bytes 98312 | tf_op jit(solution)/shard_map/ppermute | solution.py:65
  13.4 5.1 %collective-permute-start.2 = (bf16[8,16,128]{2,1,0:T(8,128)(2,1)S(1)}, bf16[8,16,128]{2,1,0:T(8,128)(2,1)S(1)}, u32[]{:S(2)}, u32[]{:S(2)}) collective-permute-start(bf16[8,16,128]{2,1,0:T(8,128)(2,1)S(1)} %collective-permute-done.1), channel_id=1, source_target_pairs={{0,1},{1,2},{2,3},{3,4},{4,5},{5,6},{6,7},{7,0},{8,9},{9,10},{10,1... | collective-permute-start | bytes 98312 | tf_op jit(solution)/shard_map/ppermute | solution.py:65
  18.6 5.1 %collective-permute-start.3 = (bf16[8,16,128]{2,1,0:T(8,128)(2,1)S(1)}, bf16[8,16,128]{2,1,0:T(8,128)(2,1)S(1)}, u32[]{:S(2)}, u32[]{:S(2)}) collective-permute-start(bf16[8,16,128]{2,1,0:T(8,128)(2,1)S(1)} %collective-permute-done.2), channel_id=1, source_target_pairs={{0,1},{1,2},{2,3},{3,4},{4,5},{5,6},{6,7},{7,0},{8,9},{9,10},{10,1... | collective-permute-start | bytes 98312 | tf_op jit(solution)/shard_map/ppermute | solution.py:65
  23.7 14.6 %collective-permute-start.4 = (bf16[8,16,128]{2,1,0:T(8,128)(2,1)S(1)}, bf16[8,16,128]{2,1,0:T(8,128)(2,1)S(1)}, u32[]{:S(2)}, u32[]{:S(2)}) collective-permute-start(bf16[8,16,128]{2,1,0:T(8,128)(2,1)S(1)} %collective-permute-done.3), channel_id=1, source_target_pairs={{0,1},{1,2},{2,3},{3,4},{4,5},{5,6},{6,7},{7,0},{8,9},{9,10},{10,1... | collective-permute-start | bytes 98312 | tf_op jit(solution)/shard_map/ppermute | solution.py:65
  38.3 17.4 %collective-permute-start.5 = (bf16[8,16,128]{2,1,0:T(8,128)(2,1)S(1)}, bf16[8,16,128]{2,1,0:T(8,128)(2,1)S(1)}, u32[]{:S(2)}, u32[]{:S(2)}) collective-permute-start(bf16[8,16,128]{2,1,0:T(8,128)(2,1)S(1)} %collective-permute-done.4), channel_id=1, source_target_pairs={{0,1},{1,2},{2,3},{3,4},{4,5},{5,6},{6,7},{7,0},{8,9},{9,10},{10,1... | collective-permute-start | bytes 98312 | tf_op jit(solution)/shard_map/ppermute | solution.py:65
  55.8 5.2 %collective-permute-start.6 = (bf16[8,16,128]{2,1,0:T(8,128)(2,1)S(1)}, bf16[8,16,128]{2,1,0:T(8,128)(2,1)S(1)}, u32[]{:S(2)}, u32[]{:S(2)}) collective-permute-start(bf16[8,16,128]{2,1,0:T(8,128)(2,1)S(1)} %collective-permute-done.5), channel_id=1, source_target_pairs={{0,1},{1,2},{2,3},{3,4},{4,5},{5,6},{6,7},{7,0},{8,9},{9,10},{10,1... | collective-permute-start | bytes 98312 | tf_op jit(solution)/shard_map/ppermute | solution.py:65
  62.9 0.8 copy-start.6
  64.0 0.8 copy-start.7
  73.5 0.8 copy-start.8
  84.3 0.8 copy-start.2
